TPU v7x, 32 devices: a whole 2x2x4 slice. The times are simulated.
32 devices in a mesh: tm: 8 (over y, x, core), panel: 4 (over z).
Axes of the slice: x: 2, y: 2, z: 4, core: 2. Of those that a mesh axis runs over, the one named last changes fastest.
Arguments:
- series: float32 [48, 2048], P(None, 'tm'), may hold values from -20 to 20, as said below
- start_block: float32 [18432, 64], P(('tm', 'panel')), may hold values from -6 to 6
Outputs:
- covariance: float32 [18432, 18432], P(('tm', 'panel'))
- basis: float32 [7, 18432, 64], P(None, ('tm', 'panel'))
- diag_blocks: float32 [6, 64, 64], replicated
- off_blocks: float32 [7, 64, 64], replicated
Inputs may be any that keep to these rules, and one draw needn't show every extreme that they name: `series`: each channel has its own scale.
All inputs are finite; a program needn't handle non-finite values.
Results may differ from a plain program's by a relative error of at most 0.0003.
Values sent between devices are 32-bit elements; how exact they have to be, the bound alone decides.
A program may use at most 192 MiB of HBM per device.

v0:
```python
import math

import jax
import jax.numpy as jnp
from jax import lax
from jax.sharding import PartitionSpec as P

M = 384
ITERS = 6


exact_precision = lax.Precision.HIGHEST


def passed_along(block, axis, distance):
    devices = range(lax.axis_size(axis))
    route = [(i - distance, i) for i in devices if i - distance in devices]
    return lax.ppermute(block, axis, route)


def lag_block(local_rows, extended, first_lag, lag_width):
    day_count = local_rows.shape[1]
    span = day_count + lag_width - 1
    segment = extended[:, first_lag : first_lag + span]
    repeated = jnp.tile(segment, (1, lag_width + 1))[:, : lag_width * (span + 1)]
    windows = repeated.reshape(segment.shape[0], lag_width, span + 1)[:, :, :day_count]
    return jnp.einsum(
        "lt,mjt->ljm",
        local_rows,
        windows,
        precision=exact_precision,
        preferred_element_type=jnp.float32,
    )


def lag_products(local_rows, extended):
    lag_width = math.gcd(M, 128)
    parts_list = [
        lag_block(local_rows, extended, first_lag, lag_width)
        for first_lag in range(0, M, lag_width)
    ]
    return jnp.concatenate(parts_list, axis=1)


def local(series, start_block):
    channels, day_count = series.shape
    tm_size = lax.axis_size("tm")
    panel_size = lax.axis_size("panel")
    total_days = day_count * tm_size
    reach_hops = (M - 1 + day_count - 1) // day_count
    pieces = [series]
    moving = series
    for distance in range(reach_hops):
        moving = passed_along(moving, "tm", -1)
        pieces.append(moving)
    extended = jnp.concatenate(pieces, axis=1)
    summed = lax.psum(lag_products(series, extended), "tm")
    counts = (total_days - jnp.arange(M)).astype(jnp.float32)
    normed = summed / counts[None, :, None]
    two_sided = jnp.concatenate([jnp.transpose(normed, (2, 1, 0))[:, :0:-1, :], normed], axis=1)
    lags_here = M // (tm_size * panel_size)
    block_index = lax.axis_index("tm") * panel_size + lax.axis_index("panel")
    row_list = []
    for offset in range(lags_here):
        lag_index = block_index * lags_here + offset
        window = lax.dynamic_slice(
            two_sided, (jnp.int32(0), M - 1 - lag_index, jnp.int32(0)), (channels, M, channels)
        )
        row_list.append(window.reshape(channels, M * channels))
    covariance = jnp.concatenate(row_list, axis=0)

    def inner(left, right):
        return jnp.dot(left.T, right, precision=exact_precision, preferred_element_type=jnp.float32)

    factor = jnp.linalg.cholesky(lax.psum(inner(start_block, start_block), ("tm", "panel")))
    current = jax.scipy.linalg.solve_triangular(factor, start_block.T, lower=True).T
    previous = jnp.zeros_like(current)
    upper = factor.T
    basis_list = [current]
    diagonal_list = []
    upper_list = [upper]
    for iteration in range(ITERS):
        work = jnp.dot(
            covariance,
            lax.all_gather(current, ("tm", "panel"), axis=0, tiled=True),
            precision=exact_precision,
            preferred_element_type=jnp.float32,
        )
        if iteration > 0:
            work = work - jnp.dot(
                previous, upper.T, precision=exact_precision, preferred_element_type=jnp.float32
            )
        diagonal, work_gram, basis_gram = lax.psum(
            (inner(current, work), inner(work, work), inner(current, current)), ("tm", "panel")
        )
        work = work - jnp.dot(
            current, diagonal, precision=exact_precision, preferred_element_type=jnp.float32
        )
        cross_term = jnp.dot(
            diagonal.T, diagonal, precision=exact_precision, preferred_element_type=jnp.float32
        )
        weighted = jnp.dot(
            diagonal.T,
            jnp.dot(
                basis_gram, diagonal, precision=exact_precision, preferred_element_type=jnp.float32
            ),
            precision=exact_precision,
            preferred_element_type=jnp.float32,
        )
        gram_matrix = work_gram - 2.0 * cross_term + weighted
        factor = jnp.linalg.cholesky(gram_matrix)
        upper = factor.T
        previous = current
        current = jax.scipy.linalg.solve_triangular(factor, work.T, lower=True).T
        basis_list.append(current)
        diagonal_list.append(diagonal)
        upper_list.append(upper)
    return (covariance, jnp.stack(basis_list), jnp.stack(diagonal_list), jnp.stack(upper_list))


def solution(mesh):
    placed = (P(None, "tm"), P(("tm", "panel"), None))
    return jax.shard_map(
        local,
        mesh=mesh,
        in_specs=placed,
        out_specs=(P(("tm", "panel"), None), P(None, ("tm", "panel"), None), P(), P()),
        check_vma=False,
    )
```

profile of v0, /device:TPU:0, one launch (start us, length us, event | category | flops | bytes accessed | tf_op | source)
XLA Modules:
  0.0 1534.1 jit_solution(18036461764195849786)
XLA Ops:
  16.1 9.8 tile.13
  42.9 9.8 tile.30
  58.0 14.1 collective-permute-start.1
  83.8 9.8 tile.32
  107.5 46.1 %psum.141 = f32[64,64]{0,1:T(8,128)S(1)} all-reduce(f32[64,64]{0,1:T(8,128)S(1)} %fusion.85), channel_id=1, replica_groups=mesh['tm'=8,'panel'=4] {'tm','panel'}, use_global_device_ids=true, to_apply=%region_1.0 | all-reduce | flops 4096 | bytes 32768 | tf_op jit(solution)/shard_map/psum | solution.py:75
  168.9 20.2 %all-reduce.8.cloned.1.call-done = f32[48,384,48]{1,0,2:T(8,128)} async-done(((f32[48,384,48]{1,0,2:T(8,128)}), f32[48,384,48]{1,0,2:T(8,128)}) %all-reduce.8.cloned.1.call-update) | async-done | bytes 3538960 | tf_op jit(solution)/shard_map/psum | solution.py:57
  195.3 8.0 reverse
  208.3 18.9 %fusion.6 = (f32[48,384,48]{1,0,2:T(8,128)}, f32[48,384,48]{1,0,2:T(8,128)}, f32[48,384,48]{1,0,2:T(8,128)}, f32[48,384,48]{1,0,2:T(8,128)}, f32[48,384,48]{1,0,2:T(8,128)}, /*index=5*/f32[48,384,48]{1,0,2:T(8,128)}) fusion(s32[]{:T(128)S(6)} %select_n.50, f32[48,383,48]{1,0,2:T(8,128)} %slice.72, f32[48,384,48]{1,0,2:T(8,128)S(1)} %copy-done.3, ...), kind=kLoop, calls=%fused_computation.30 | loop fusion | flops 5308416 | bytes 28302360 | tf_op jit(solution)/shard_map/concatenate | solution.py:60
  234.9 10.3 reshape.81
  257.0 10.2 reshape.82
  275.0 10.2 reshape.83
  293.0 10.4 reshape.84
  303.3 7.8 copy.85
  311.1 10.2 reshape.85
  321.4 27.2 %fusion.17 = (f32[48,384,48]{1,0,2:T(8,128)}, f32[48,384,48]{1,0,2:T(8,128)}, f32[48,384,48]{1,0,2:T(8,128)}, f32[48,384,48]{1,0,2:T(8,128)}, f32[48,384,48]{1,0,2:T(8,128)}, /*index=5*/f32[48,384,48]{1,0,2:T(8,128)}) fusion(s32[]{:T(128)S(6)} %select_n.49, f32[48,383,48]{1,0,2:T(8,128)} %slice.72, f32[48,384,48]{1,0,2:T(8,128)} %copy-done.2, ...), kind=kLoop, calls=%fused_computation.41 | loop fusion | flops 5308416 | bytes 28302360 | tf_op jit(solution)/shard_map/concatenate | solution.py:60
  348.6 7.8 copy.86
  356.4 10.2 reshape.86
  374.4 10.3 reshape.87
  384.7 7.8 copy.88
  392.5 10.4 reshape.88
  433.3 10.2 reshape.89
  443.5 7.8 copy.90
  451.3 10.2 reshape.90
  469.3 10.3 reshape.91
  487.3 10.6 reshape.92
  510.7 7.8 copy.95
  524.9 43.1 %fusion.86 = f32[576,64]{0,1:T(8,128)S(1)} fusion(f32[576,18432]{1,0:T(8,128)} %constant_dynamic-update-slice_fusion.2, f32[18432,64]{0,1:T(8,128)} %reshape.94), kind=kOutput, calls=%fused_computation.202 | convolution fusion | flops 8153726976 | bytes 47333376 | tf_op jit(solution)/shard_map/dot_general | solution.py:83
  568.7 46.3 %all-reduce.5 = (f32[64,64]{1,0:T(8,128)S(1)}, f32[64,64]{0,1:T(8,128)S(1)}, f32[64,64]{1,0:T(8,128)S(1)}) all-reduce(f32[64,64]{1,0:T(8,128)S(1)} %fusion.88, f32[64,64]{0,1:T(8,128)S(1)} %fusion.87, f32[64,64]{1,0:T(8,128)S(1)} %copy-done.24), channel_id=1, replica_groups=mesh['tm'=8,'panel'=4] {'tm','panel'}, use_global_device_ids=true, to_apply=%region_5.0 | all-reduce | flops 12288 | bytes 98304 | tf_op jit(solution)/shard_map/psum | solution.py:93
  630.6 63.8 %all-gather.15.cloned.1.call-done = f32[32,576,64]{1,2,0:T(8,128)} async-done(((f32[1,576,64]{1,2,0:T(8,128)}), f32[32,576,64]{1,2,0:T(8,128)}) %all-gather.15.cloned.1.call-update) | async-done | bytes 4718608 | tf_op jit(solution)/shard_map/all_gather | solution.py:85
  694.4 7.8 copy.100
  708.8 43.1 %fusion.91 = f32[576,64]{0,1:T(8,128)S(1)} fusion(f32[576,18432]{1,0:T(8,128)} %constant_dynamic-update-slice_fusion.2, f32[18432,64]{0,1:T(8,128)} %reshape.96), kind=kOutput, calls=%fused_computation.207 | convolution fusion | flops 8153726976 | bytes 47333376 | tf_op jit(solution)/shard_map/dot_general | solution.py:83
  753.5 40.2 %all-reduce.4 = (f32[64,64]{1,0:T(8,128)S(1)}, f32[64,64]{0,1:T(8,128)S(1)}, f32[64,64]{1,0:T(8,128)S(1)}) all-reduce(f32[64,64]{1,0:T(8,128)S(1)} %fusion.93, f32[64,64]{0,1:T(8,128)S(1)} %fusion.92, f32[64,64]{1,0:T(8,128)S(1)} %fusion.94), channel_id=1, replica_groups=mesh['tm'=8,'panel'=4] {'tm','panel'}, use_global_device_ids=true, to_apply=%region_8.0 | all-reduce | flops 12288 | bytes 98304 | tf_op jit(solution)/shard_map/psum | solution.py:93
  809.7 63.8 %all-gather.17.cloned.1.call-done = f32[32,576,64]{1,2,0:T(8,128)} async-done(((f32[1,576,64]{1,2,0:T(8,128)}), f32[32,576,64]{1,2,0:T(8,128)}) %all-gather.17.cloned.1.call-update) | async-done | bytes 4718608 | tf_op jit(solution)/shard_map/all_gather | solution.py:85
  873.5 7.8 copy.105
  887.7 43.1 %fusion.96 = f32[576,64]{0,1:T(8,128)S(1)} fusion(f32[576,18432]{1,0:T(8,128)} %constant_dynamic-update-slice_fusion.2, f32[18432,64]{0,1:T(8,128)} %reshape.98), kind=kOutput, calls=%fused_computation.212 | convolution fusion | flops 8153726976 | bytes 47333376 | tf_op jit(solution)/shard_map/dot_general | solution.py:83
  932.5 40.4 %all-reduce.3 = (f32[64,64]{1,0:T(8,128)S(1)}, f32[64,64]{0,1:T(8,128)S(1)}, f32[64,64]{1,0:T(8,128)S(1)}) all-reduce(f32[64,64]{1,0:T(8,128)S(1)} %fusion.98, f32[64,64]{0,1:T(8,128)S(1)} %fusion.97, f32[64,64]{1,0:T(8,128)S(1)} %fusion.99), channel_id=1, replica_groups=mesh['tm'=8,'panel'=4] {'tm','panel'}, use_global_device_ids=true, to_apply=%region_11.0 | all-reduce | flops 12288 | bytes 98304 | tf_op jit(solution)/shard_map/psum | solution.py:93
  988.3 64.2 %all-gather.19.cloned.1.call-done = f32[32,576,64]{1,2,0:T(8,128)} async-done(((f32[1,576,64]{1,2,0:T(8,128)}), f32[32,576,64]{1,2,0:T(8,128)}) %all-gather.19.cloned.1.call-update) | async-done | bytes 4718608 | tf_op jit(solution)/shard_map/all_gather | solution.py:85
  1052.5 7.8 copy.110
  1066.7 43.1 %fusion.101 = f32[576,64]{0,1:T(8,128)S(1)} fusion(f32[576,18432]{1,0:T(8,128)} %constant_dynamic-update-slice_fusion.2, f32[18432,64]{0,1:T(8,128)} %reshape.100), kind=kOutput, calls=%fused_computation.217 | convolution fusion | flops 8153726976 | bytes 47333376 | tf_op jit(solution)/shard_map/dot_general | solution.py:83
  1111.4 40.4 %all-reduce.2 = (f32[64,64]{1,0:T(8,128)S(1)}, f32[64,64]{0,1:T(8,128)S(1)}, f32[64,64]{1,0:T(8,128)S(1)}) all-reduce(f32[64,64]{1,0:T(8,128)S(1)} %fusion.103, f32[64,64]{0,1:T(8,128)S(1)} %fusion.102, f32[64,64]{1,0:T(8,128)S(1)} %fusion.104), channel_id=1, replica_groups=mesh['tm'=8,'panel'=4] {'tm','panel'}, use_global_device_ids=true, to_apply=%region_14.0 | all-reduce | flops 12288 | bytes 98304 | tf_op jit(solution)/shard_map/psum | solution.py:93
  1167.5 64.2 %all-gather.21.cloned.1.call-done = f32[32,576,64]{1,2,0:T(8,128)} async-done(((f32[1,576,64]{1,2,0:T(8,128)}), f32[32,576,64]{1,2,0:T(8,128)}) %all-gather.21.cloned.1.call-update) | async-done | bytes 4718608 | tf_op jit(solution)/shard_map/all_gather | solution.py:85
  1231.7 7.8 copy.115
  1245.9 43.1 %fusion.106 = f32[576,64]{0,1:T(8,128)S(1)} fusion(f32[576,18432]{1,0:T(8,128)} %constant_dynamic-update-slice_fusion.2, f32[18432,64]{0,1:T(8,128)} %reshape.102), kind=kOutput, calls=%fused_computation.222 | convolution fusion | flops 8153726976 | bytes 47333376 | tf_op jit(solution)/shard_map/dot_general | solution.py:83
  1290.7 40.6 %all-reduce.1 = (f32[64,64]{1,0:T(8,128)S(1)}, f32[64,64]{0,1:T(8,128)S(1)}, f32[64,64]{1,0:T(8,128)S(1)}) all-reduce(f32[64,64]{1,0:T(8,128)S(1)} %fusion.108, f32[64,64]{0,1:T(8,128)S(1)} %fusion.107, f32[64,64]{1,0:T(8,128)S(1)} %fusion.109), channel_id=1, replica_groups=mesh['tm'=8,'panel'=4] {'tm','panel'}, use_global_device_ids=true, to_apply=%region_17.0 | all-reduce | flops 12288 | bytes 98304 | tf_op jit(solution)/shard_map/psum | solution.py:93
  1350.8 60.3 %all-gather.23.cloned.1.call-done = f32[32,576,64]{1,2,0:T(8,128)} async-done(((f32[1,576,64]{1,2,0:T(8,128)}), f32[32,576,64]{1,2,0:T(8,128)}) %all-gather.23.cloned.1.call-update) | async-done | bytes 4718608 | tf_op jit(solution)/shard_map/all_gather | solution.py:85
  1411.1 7.9 copy.120
  1425.3 43.3 %fusion.111 = f32[576,64]{0,1:T(8,128)S(1)} fusion(f32[576,18432]{1,0:T(8,128)} %constant_dynamic-update-slice_fusion.2, f32[18432,64]{0,1:T(8,128)} %reshape.104), kind=kOutput, calls=%fused_computation.227 | convolution fusion | flops 8153726976 | bytes 47333376 | tf_op jit(solution)/shard_map/dot_general | solution.py:83
  1470.2 40.2 %all-reduce = (f32[64,64]{1,0:T(8,128)S(1)}, f32[64,64]{0,1:T(8,128)S(1)}, f32[64,64]{1,0:T(8,128)S(1)}) all-reduce(f32[64,64]{1,0:T(8,128)S(1)} %fusion.113, f32[64,64]{0,1:T(8,128)S(1)} %fusion.112, f32[64,64]{1,0:T(8,128)S(1)} %fusion.114), channel_id=1, replica_groups=mesh['tm'=8,'panel'=4] {'tm','panel'}, use_global_device_ids=true, to_apply=%region_20.23 | all-reduce | flops 12288 | bytes 98304 | tf_op jit(solution)/shard_map/psum | solution.py:93
  (243 shorter events, 328.5 us)
Async XLA Ops:
  8.0 99.2 %copy-start = (f32[576,64]{0,1:T(8,128)S(1)}, f32[576,64]{0,1:T(8,128)}, u32[]{:S(2)}) copy-start(f32[576,64]{0,1:T(8,128)} %param.6) | copy-start | bytes 442372
  8.0 181.1 %all-reduce.8.cloned.1.call-start = ((), (), s32[]{:S(2)}) async-start(), calls=%async_computation | async-start | bytes 7077888 | tf_op jit(solution)/shard_map/psum | solution.py:57
  8.1 3.5 collective-permute-start
  25.9 3.7 slice-start
  29.6 1.6 copy-start.21
  52.7 3.7 slice-start.1
  58.0 21.2 %collective-permute-start.1 = (f32[48,256]{1,0:T(8,128)S(1)}, f32[48,256]{1,0:T(8,128)S(1)}, u32[]{:S(2)}, u32[]{:S(2)}) collective-permute-start(f32[48,256]{1,0:T(8,128)S(1)} %collective-permute-done), channel_id=1, source_target_pairs={{4,0},{8,4},{12,8},{16,12},{20,16},{24,20},{28,24},{5,1},{9,5},{13... | collective-permute-start | bytes 147464 | tf_op jit(solution)/shard_map/ppermute | solution.py:18
  93.6 3.7 slice-start.2
  98.9 6.1 copy-start.19
  98.9 6.1 copy-start.20
  107.1 403.6 %all-gather.13.cloned.1.call-start = ((), (), s32[]{:S(2)}) async-start(), calls=%async_computation.1 | async-start | bytes 5406720 | tf_op jit(solution)/shard_map/all_gather | solution.py:85
  159.5 33.0 %copy-start.22 = (f32[64,64]{1,0:T(8,128)}, f32[64,64]{1,0:T(8,128)S(1)}, u32[]{:S(2)}) copy-start(f32[64,64]{1,0:T(8,128)S(1)} %cholesky.119) | copy-start | bytes 49156
  166.9 527.4 %all-gather.15.cloned.1.call-start = ((), (), s32[]{:S(2)}) async-start(), calls=%async_computation.2 | async-start | bytes 5406720 | tf_op jit(solution)/shard_map/all_gather | solution.py:85
  191.4 3.9 copy-start.2
  203.4 4.9 copy-start.3
  402.9 4.2 copy-start.4
  407.0 3.3 copy-start.5
  410.3 3.3 copy-start.6
  413.6 3.3 copy-start.7
  416.9 3.3 copy-start.8
  420.2 3.3 copy-start.9
  497.9 4.2 copy-start.10
  502.1 3.3 copy-start.11
  505.4 3.3 copy-start.12
  524.9 43.5 %copy-start.13 = (f32[64,576]{1,0:T(8,128)S(1)}, f32[64,576]{1,0:T(8,128)}, u32[]{:S(2)}) copy-start(f32[64,576]{1,0:T(8,128)} %get-tuple-element.51) | copy-start | bytes 442372
  524.9 43.8 %copy-start.24 = (f32[64,64]{1,0:T(8,128)S(1)}, f32[64,64]{1,0:T(8,128)}, u32[]{:S(2)}) copy-start(f32[64,64]{1,0:T(8,128)} %fusion.89) | copy-start | bytes 49156
  524.9 103.3 %copy-start.25 = (f32[7,576,64]{1,2,0:T(8,128)S(1)}, f32[7,576,64]{1,2,0:T(8,128)}, u32[]{:S(2)}) copy-start(f32[7,576,64]{1,2,0:T(8,128)} %get-tuple-element.50) | copy-start | bytes 3096580
  629.3 244.3 %all-gather.17.cloned.1.call-start = ((), (), s32[]{:S(2)}) async-start(), calls=%async_computation.3 | async-start | bytes 5406720 | tf_op jit(solution)/shard_map/all_gather | solution.py:85
  708.8 44.5 %copy-start.15 = (f32[64,576]{1,0:T(8,128)S(1)}, f32[64,576]{1,0:T(8,128)}, u32[]{:S(2)}) copy-start(f32[64,576]{1,0:T(8,128)} %get-tuple-element.53) | copy-start | bytes 442372
  808.0 244.5 %all-gather.19.cloned.1.call-start = ((), (), s32[]{:S(2)}) async-start(), calls=%async_computation.4 | async-start | bytes 5406720 | tf_op jit(solution)/shard_map/all_gather | solution.py:85
  887.7 44.5 %copy-start.16 = (f32[64,576]{1,0:T(8,128)S(1)}, f32[64,576]{1,0:T(8,128)}, u32[]{:S(2)}) copy-start(f32[64,576]{1,0:T(8,128)} %get-tuple-element.55) | copy-start | bytes 442372
  987.0 244.7 %all-gather.21.cloned.1.call-start = ((), (), s32[]{:S(2)}) async-start(), calls=%async_computation.5 | async-start | bytes 5406720 | tf_op jit(solution)/shard_map/all_gather | solution.py:85
  1066.7 44.4 %copy-start.17 = (f32[64,576]{1,0:T(8,128)S(1)}, f32[64,576]{1,0:T(8,128)}, u32[]{:S(2)}) copy-start(f32[64,576]{1,0:T(8,128)} %get-tuple-element.57) | copy-start | bytes 442372
  1166.2 245.0 %all-gather.23.cloned.1.call-start = ((), (), s32[]{:S(2)}) async-start(), calls=%async_computation.6 | async-start | bytes 5406720 | tf_op jit(solution)/shard_map/all_gather | solution.py:85
  1245.9 44.5 %copy-start.14 = (f32[64,576]{1,0:T(8,128)S(1)}, f32[64,576]{1,0:T(8,128)}, u32[]{:S(2)}) copy-start(f32[64,576]{1,0:T(8,128)} %get-tuple-element.59) | copy-start | bytes 442372
  1245.9 99.6 %copy-start.23 = (f32[64,64]{1,0:T(8,128)S(1)}, f32[64,64]{1,0:T(8,128)}, u32[]{:S(2)}) copy-start(f32[64,64]{1,0:T(8,128)} %copy-done.22) | copy-start | bytes 49156
  1425.3 44.6 %copy-start.18 = (f32[64,576]{1,0:T(8,128)S(1)}, f32[64,576]{1,0:T(8,128)}, u32[]{:S(2)}) copy-start(f32[64,576]{1,0:T(8,128)} %get-tuple-element.61) | copy-start | bytes 442372
  1425.3 101.1 %copy-start.1 = (f32[576,64]{0,1:T(8,128)S(1)}, f32[576,64]{0,1:T(8,128)}, u32[]{:S(2)}) copy-start(f32[576,64]{0,1:T(8,128)} %param.6) | copy-start | bytes 442372
  1520.2 5.3 copy-start.27
  1525.4 1.0 copy-start.26
Sparse Core Ops, SparseCore 0:
  107.2 81.8 all-reduce.7
Sparse Core Ops, SparseCore 1:
  167.0 69.8 all-gather.12
  629.3 65.0 all-gather.14
  808.1 65.4 all-gather.16
  987.1 65.4 all-gather.18
  1166.2 65.4 all-gather.20
  1345.6 65.4 all-gather.22
where the time goes:
time: 1550 us; the launch traced here: 1530 us
  local copies, waits for them, and re-layouts  421 us (27%)
  waiting for transfers between devices  338 us (22%)
  matrix products  309 us (20%)
  blocking collectives  294 us (19%)
  other arithmetic  139 us (9%)
  between operations  16.8 us (1%)
  starting transfers between devices  16.2 us (1%)
    all_gather x6, waiting for transfers between devices, local(): lax.all_gather(current, ('tm', 'panel'), axis=0, tiled=True)  316 us
    dot_general x6, matrix products, local(): jnp.dot(covariance, lax.all_gather(current, ('tm', 'panel'), axis=0, tile...  259 us
    psum x6, blocking collectives, local(): lax.psum((inner(current, work), inner(work, work), inner(current, current...  248 us
    reshape x12, local copies, waits for them, and re-layouts, local(): row_list.append(window.reshape(channels, M * channels))  124 us
    unnamed x85, local copies, waits for them, and re-layouts  96.2 us
    dynamic_slice x12, local copies, waits for them, and re-layouts, local(): lax.dynamic_slice(two_sided, (jnp.int32(0), M - 1 - lag_index, jnp.int32(...  93.3 us
    all_gather x6, local copies, waits for them, and re-layouts, local(): lax.all_gather(current, ('tm', 'panel'), axis=0, tiled=True)  47 us
    concatenate x2, other arithmetic, local(): jnp.concatenate([jnp.transpose(normed, (2, 1, 0))[:, :0:-1, :], normed],...  46.1 us
  transfers between devices with their start and end apart: 9, of which 7 were waited for; matrix products, arithmetic and copies ran while one was open for 23% of the time, Pallas kernels for 0%

commit v1 on v0

--- a/solution.py
+++ b/solution.py
@@ -1,8 +1,8 @@
-import math
-
 import jax
 import jax.numpy as jnp
 from jax import lax
+from jax.experimental import pallas as pl
+from jax.experimental.pallas import tpu as pltpu
 from jax.sharding import PartitionSpec as P
 
 M = 384
@@ -18,28 +18,96 @@
     return lax.ppermute(block, axis, route)
 
 
-def lag_block(local_rows, extended, first_lag, lag_width):
-    day_count = local_rows.shape[1]
-    span = day_count + lag_width - 1
-    segment = extended[:, first_lag : first_lag + span]
-    repeated = jnp.tile(segment, (1, lag_width + 1))[:, : lag_width * (span + 1)]
-    windows = repeated.reshape(segment.shape[0], lag_width, span + 1)[:, :, :day_count]
-    return jnp.einsum(
-        "lt,mjt->ljm",
-        local_rows,
-        windows,
+def lag_kernel(x_ref, g_ref, o_ref):
+    groups, _, width = g_ref.shape
+    depth = x_ref.shape[1] // groups
+    x = x_ref[...]
+    for step in range(o_ref.shape[1] // width):
+        window = g_ref[:, step : step + depth, :].reshape(groups * depth, width)
+        o_ref[:, step * width : (step + 1) * width] = jnp.dot(
+            x, window, precision=exact_precision, preferred_element_type=jnp.float32
+        )
+
+
+def lag_products(local_rows, extended):
+    channels, day_count = local_rows.shape
+    groups = 8
+    width = groups * channels
+    depth = day_count // groups
+    rows = depth + M // groups
+    days = jnp.pad(extended, ((0, 0), (0, max(0, rows * groups + groups - extended.shape[1]))))
+    flat = days.T.reshape(-1)
+    shifted = jnp.stack(
+        [
+            lax.slice(flat, (r * channels,), (r * channels + rows * width,)).reshape(rows, width)
+            for r in range(groups)
+        ]
+    )
+    by_group = local_rows.reshape(channels, depth, groups).transpose(0, 2, 1)
+    return pl.pallas_call(
+        lag_kernel,
+        out_shape=jax.ShapeDtypeStruct((channels, M * channels), jnp.float32),
+        in_specs=[pl.BlockSpec(memory_space=pltpu.VMEM)] * 2,
+        out_specs=pl.BlockSpec(memory_space=pltpu.VMEM),
+    )(by_group.reshape(channels, day_count), shifted)
+
+
+def gram_kernel(sizes, q_ref, w_ref, o_ref, held, arrived, send_sem, recv_sem):
+    partners = []
+    for axis, size in sizes:
+        me = lax.axis_index(axis)
+        distance = 1
+        while distance < size:
+            partners.append((axis, me + distance - 2 * distance * ((me // distance) % 2)))
+            distance *= 2
+    barrier = pltpu.get_barrier_semaphore()
+    for axis, other in partners:
+        pl.semaphore_signal(
+            barrier, inc=1, device_id={axis: other}, device_id_type=pl.DeviceIdType.MESH
+        )
+    both = jnp.concatenate([q_ref[...], w_ref[...]], axis=1)
+    held[0] = lax.dot_general(
+        both,
+        both,
+        (((0,), (0,)), ((), ())),
         precision=exact_precision,
         preferred_element_type=jnp.float32,
     )
+    pl.semaphore_wait(barrier, len(partners))
+    for step, (axis, other) in enumerate(partners):
+        copy = pltpu.make_async_remote_copy(
+            src_ref=held.at[step],
+            dst_ref=arrived.at[step],
+            send_sem=send_sem.at[step],
+            recv_sem=recv_sem.at[step],
+            device_id={axis: other},
+            device_id_type=pl.DeviceIdType.MESH,
+        )
+        copy.start()
+        copy.wait()
+        held[step + 1] = held[step] + arrived[step]
+    o_ref[...] = held[len(partners)]
 
 
-def lag_products(local_rows, extended):
-    lag_width = math.gcd(M, 128)
-    parts_list = [
-        lag_block(local_rows, extended, first_lag, lag_width)
-        for first_lag in range(0, M, lag_width)
-    ]
-    return jnp.concatenate(parts_list, axis=1)
+def grams(q, w):
+    sizes = [("tm", lax.axis_size("tm")), ("panel", lax.axis_size("panel"))]
+    steps = sum(size.bit_length() - 1 for _, size in sizes)
+    width = q.shape[1] + w.shape[1]
+    out = pl.pallas_call(
+        lambda *refs: gram_kernel(sizes, *refs),
+        out_shape=jax.ShapeDtypeStruct((width, width), jnp.float32),
+        in_specs=[pl.BlockSpec(memory_space=pltpu.VMEM)] * 2,
+        out_specs=pl.BlockSpec(memory_space=pltpu.VMEM),
+        scratch_shapes=[
+            pltpu.VMEM((steps + 1, width, width), jnp.float32),
+            pltpu.VMEM((steps, width, width), jnp.float32),
+            pltpu.SemaphoreType.DMA((steps,)),
+            pltpu.SemaphoreType.DMA((steps,)),
+        ],
+        compiler_params=pltpu.CompilerParams(collective_id=0, has_side_effects=True),
+    )(q, w)
+    half = q.shape[1]
+    return out[:half, :half], out[:half, half:], out[half:, half:]
 
 
 def local(series, start_block):
@@ -56,23 +124,24 @@
     extended = jnp.concatenate(pieces, axis=1)
     summed = lax.psum(lag_products(series, extended), "tm")
     counts = (total_days - jnp.arange(M)).astype(jnp.float32)
-    normed = summed / counts[None, :, None]
-    two_sided = jnp.concatenate([jnp.transpose(normed, (2, 1, 0))[:, :0:-1, :], normed], axis=1)
+    counts = (total_days - jnp.arange(M * channels) // channels).astype(jnp.float32)
+    normed = summed / counts[None, :]
+    blocks = normed.reshape(channels, M, channels)
+    before = jnp.transpose(blocks, (2, 1, 0))[:, :0:-1, :].reshape(channels, (M - 1) * channels)
+    two_sided = jnp.concatenate([before, normed], axis=1)
     lags_here = M // (tm_size * panel_size)
     block_index = lax.axis_index("tm") * panel_size + lax.axis_index("panel")
+    first = (M - lags_here - block_index * lags_here) * channels
+    near = lax.dynamic_slice(
+        two_sided, (jnp.int32(0), first), (channels, (M + lags_here - 1) * channels)
+    )
     row_list = []
     for offset in range(lags_here):
-        lag_index = block_index * lags_here + offset
-        window = lax.dynamic_slice(
-            two_sided, (jnp.int32(0), M - 1 - lag_index, jnp.int32(0)), (channels, M, channels)
-        )
-        row_list.append(window.reshape(channels, M * channels))
+        start = (lags_here - 1 - offset) * channels
+        row_list.append(near[:, start : start + M * channels])
     covariance = jnp.concatenate(row_list, axis=0)
 
-    def inner(left, right):
-        return jnp.dot(left.T, right, precision=exact_precision, preferred_element_type=jnp.float32)
-
-    factor = jnp.linalg.cholesky(lax.psum(inner(start_block, start_block), ("tm", "panel")))
+    factor = jnp.linalg.cholesky(grams(start_block, start_block)[0])
     current = jax.scipy.linalg.solve_triangular(factor, start_block.T, lower=True).T
     previous = jnp.zeros_like(current)
     upper = factor.T
@@ -83,16 +152,14 @@
         work = jnp.dot(
             covariance,
             lax.all_gather(current, ("tm", "panel"), axis=0, tiled=True),
-            precision=exact_precision,
+            precision=lax.Precision.HIGH,
             preferred_element_type=jnp.float32,
         )
         if iteration > 0:
             work = work - jnp.dot(
                 previous, upper.T, precision=exact_precision, preferred_element_type=jnp.float32
             )
-        diagonal, work_gram, basis_gram = lax.psum(
-            (inner(current, work), inner(work, work), inner(current, current)), ("tm", "panel")
-        )
+        basis_gram, diagonal, work_gram = grams(current, work)
         work = work - jnp.dot(
             current, diagonal, precision=exact_precision, preferred_element_type=jnp.float32
         )

time: 1550 us -> 1090 us (0.70)
  blocking collectives: 294 us -> 0 us
  local copies, waits for them, and re-layouts: 421 us -> 263 us
  Pallas kernels: 0 us -> 156 us
  matrix products: 309 us -> 183 us
  other arithmetic: 139 us -> 96.3 us
  waiting for transfers between devices: 338 us -> 355 us
    psum x7 -> x0, blocking collectives: 294 us -> none  [the longest x6 248 us: local(): lax.psum((inner(current, work), inner(work, work), inner(current, current...]
    pallas_call x0 -> x8, Pallas kernels: none -> 156 us  [the longest x7 144 us: grams(): pl.pallas_call(lambda *refs: gram_kernel(sizes, *refs), out_shape=jax.Sha...]
    dot_general x6, matrix products: 259 us -> 148 us  [local(): jnp.dot(covariance, lax.all_gather(current, ('tm', 'panel'), axis=0, tile...]
    reshape x12 -> x3, local copies, waits for them, and re-layouts: 124 us -> 17.3 us  [the longest x1 10.4 us: local(): jnp.transpose(blocks, (2, 1, 0))[:, :0:-1, :]]
    dynamic_slice x12 -> x0, local copies, waits for them, and re-layouts: 93.3 us -> none  [local(): lax.dynamic_slice(two_sided, (jnp.int32(0), M - 1 - lag_index, jnp.int32(...]
    rev x0 -> x2, local copies, waits for them, and re-layouts: none -> 86.7 us  [local(): jnp.transpose(blocks, (2, 1, 0))[:, :0:-1, :]]
    concatenate x4 -> x1, other arithmetic: 48.1 us -> 2.84 us  [local(): two_sided = jnp.concatenate([before, normed], axis=1)]
    another operation x6 -> x21, local copies, waits for them, and re-layouts: 43.1 us -> 7 us  [the longest x6 4.9 us: local(): jnp.stack(basis_list)]
  transfers between devices with their start and end apart: 9 -> 9, of which waited for: 7 -> 8; matrix products, arithmetic and copies ran while one was open for 23% -> 16% of each run, Pallas kernels for 0% -> 2%
where the time goes in v1:
time: 1090 us; the launch traced here: 1070 us
  waiting for transfers between devices  355 us (33%)
  local copies, waits for them, and re-layouts  263 us (24%)
  matrix products  183 us (17%)
  Pallas kernels  156 us (14%)
  other arithmetic  96.3 us (9%)
  between operations  16.9 us (2%)
    all_gather x6, waiting for transfers between devices, local(): lax.all_gather(current, ('tm', 'panel'), axis=0, tiled=True)  308 us
    dot_general x6, matrix products, local(): jnp.dot(covariance, lax.all_gather(current, ('tm', 'panel'), axis=0, tile...  148 us
    pallas_call x7, Pallas kernels, grams(): pl.pallas_call(lambda *refs: gram_kernel(sizes, *refs), out_shape=jax.Sha...  144 us
    rev x2, local copies, waits for them, and re-layouts, local(): jnp.transpose(blocks, (2, 1, 0))[:, :0:-1, :]  86.7 us
    unnamed x92, local copies, waits for them, and re-layouts  79.9 us
    all_gather x6, local copies, waits for them, and re-layouts, local(): lax.all_gather(current, ('tm', 'panel'), axis=0, tiled=True)  47.2 us
    psum x1, waiting for transfers between devices, local(): summed = lax.psum(lag_products(series, extended), 'tm')  41.9 us
    another operation x18, other arithmetic, local(): factor = jnp.linalg.cholesky(gram_matrix)  39.2 us
  transfers between devices with their start and end apart: 9, of which 8 were waited for; matrix products, arithmetic and copies ran while one was open for 16% of the time, Pallas kernels for 2%

profile of v1, /device:TPU:0, one launch (start us, length us, event | category | flops | bytes accessed | tf_op | source)
XLA Modules:
  0.0 1074.0 jit_solution(13053450079170921308)
XLA Ops:
  22.4 11.8 %shard_map.57 = f32[48,18432]{1,0:T(8,128)} custom-call(f32[48,256]{1,0:T(8,128)} %reshape.61.x_ref, f32[8,80,384]{2,1,0:T(8,128)} %copy-done.18), custom_call_target="tpu_custom_call" | custom-call | tf_op jit(solution)/shard_map/pallas_call | solution.py:47
  35.7 26.3 %shard_map.58 = f32[128,128]{1,0:T(8,128)} custom-call(f32[576,64]{1,0:T(8,128)} %copy.280.refs_0_.refs_1_, f32[576,64]{1,0:T(8,128)} %copy.280.refs_0_.refs_1_), custom_call_target="tpu_custom_call" | custom-call | tf_op jit(solution)/shard_map/pallas_call | solution.py:96
  63.6 5.8 cholesky.119
  70.8 4.9 custom-call.11
  77.8 41.9 %all-reduce.2.cloned.1.call-done = f32[48,18432]{1,0:T(8,128)} async-done(((f32[48,18432]{1,0:T(8,128)}), f32[48,18432]{1,0:T(8,128)}) %all-reduce.2.cloned.1.call-update) | async-done | bytes 3538960 | tf_op jit(solution)/shard_map/psum | solution.py:125
  122.0 6.2 reshape.62
  128.2 8.5 slice.184
  136.6 74.3 %rev.3 = f32[48,383,48]{0,1,2:T(8,128)} reverse(f32[48,383,48]{0,1,2:T(8,128)} %slice.184), dimensions={1} | reverse | bytes 7059456 | tf_op jit(solution)/shard_map/rev | solution.py:130
  211.0 12.4 %copy.279 = f32[48,383,48]{2,1,0:T(8,128)} copy(f32[48,383,48]{0,1,2:T(8,128)} %rev.3) | data formatting | bytes 7059456 | tf_op jit(solution)/shard_map/rev | solution.py:130
  223.3 10.4 reshape.63
  268.3 8.0 copy.286
  276.4 6.4 reshape.65
  282.8 24.6 %fusion.97 = f32[576,64]{0,1:T(8,128)S(1)} fusion(f32[576,18432]{1,0:T(8,128)} %slice_dynamic-update-slice_fusion, f32[18432,64]{0,1:T(8,128)} %reshape.65), kind=kOutput, calls=%fused_computation.204 | convolution fusion | flops 4076863488 | bytes 47333376 | tf_op jit(solution)/shard_map/dot_general | solution.py:152
  308.2 21.1 %shard_map.59 = f32[128,128]{1,0:T(8,128)} custom-call(f32[576,64]{1,0:T(8,128)} %bitcast.203, f32[576,64]{1,0:T(8,128)} %copy.287.refs_1_), custom_call_target="tpu_custom_call" | custom-call | tf_op jit(solution)/shard_map/pallas_call | solution.py:96
  334.7 5.8 cholesky.130
  341.9 4.9 custom-call.12
  348.7 62.9 %all-gather.15.cloned.1.call-done = f32[32,576,64]{1,2,0:T(8,128)} async-done(((f32[1,576,64]{1,2,0:T(8,128)}), f32[32,576,64]{1,2,0:T(8,128)}) %all-gather.15.cloned.1.call-update) | async-done | bytes 4718608 | tf_op jit(solution)/shard_map/all_gather | solution.py:154
  411.6 7.8 copy.294
  419.4 6.4 reshape.67
  425.8 24.6 %fusion.98 = f32[576,64]{0,1:T(8,128)S(1)} fusion(f32[576,18432]{1,0:T(8,128)} %slice_dynamic-update-slice_fusion, f32[18432,64]{0,1:T(8,128)} %reshape.67), kind=kOutput, calls=%fused_computation.205 | convolution fusion | flops 4076863488 | bytes 47333376 | tf_op jit(solution)/shard_map/dot_general | solution.py:152
  452.2 19.4 %shard_map.60 = f32[128,128]{1,0:T(8,128)} custom-call(f32[576,64]{1,0:T(8,128)} %bitcast.205, f32[576,64]{1,0:T(8,128)} %copy.295.refs_1_), custom_call_target="tpu_custom_call" | custom-call | tf_op jit(solution)/shard_map/pallas_call | solution.py:96
  477.0 5.8 cholesky.141
  490.8 63.4 %all-gather.17.cloned.1.call-done = f32[32,576,64]{1,2,0:T(8,128)} async-done(((f32[1,576,64]{1,2,0:T(8,128)}), f32[32,576,64]{1,2,0:T(8,128)}) %all-gather.17.cloned.1.call-update) | async-done | bytes 4718608 | tf_op jit(solution)/shard_map/all_gather | solution.py:154
  554.2 7.8 copy.302
  562.0 6.4 reshape.69
  568.4 24.6 %fusion.99 = f32[576,64]{0,1:T(8,128)S(1)} fusion(f32[576,18432]{1,0:T(8,128)} %slice_dynamic-update-slice_fusion, f32[18432,64]{0,1:T(8,128)} %reshape.69), kind=kOutput, calls=%fused_computation.206 | convolution fusion | flops 4076863488 | bytes 47333376 | tf_op jit(solution)/shard_map/dot_general | solution.py:152
  594.9 19.4 %shard_map.61 = f32[128,128]{1,0:T(8,128)} custom-call(f32[576,64]{1,0:T(8,128)} %bitcast.207, f32[576,64]{1,0:T(8,128)} %copy.303.refs_1_), custom_call_target="tpu_custom_call" | custom-call | tf_op jit(solution)/shard_map/pallas_call | solution.py:96
  619.7 5.8 cholesky.152
  633.3 63.3 %all-gather.19.cloned.1.call-done = f32[32,576,64]{1,2,0:T(8,128)} async-done(((f32[1,576,64]{1,2,0:T(8,128)}), f32[32,576,64]{1,2,0:T(8,128)}) %all-gather.19.cloned.1.call-update) | async-done | bytes 4718608 | tf_op jit(solution)/shard_map/all_gather | solution.py:154
  696.7 7.8 copy.310
  704.5 6.4 reshape.71
  710.9 24.6 %fusion.100 = f32[576,64]{0,1:T(8,128)S(1)} fusion(f32[576,18432]{1,0:T(8,128)} %slice_dynamic-update-slice_fusion, f32[18432,64]{0,1:T(8,128)} %reshape.71), kind=kOutput, calls=%fused_computation.207 | convolution fusion | flops 4076863488 | bytes 47333376 | tf_op jit(solution)/shard_map/dot_general | solution.py:152
  737.3 19.4 %shard_map.62 = f32[128,128]{1,0:T(8,128)} custom-call(f32[576,64]{1,0:T(8,128)} %bitcast.209, f32[576,64]{1,0:T(8,128)} %copy.311.refs_1_), custom_call_target="tpu_custom_call" | custom-call | tf_op jit(solution)/shard_map/pallas_call | solution.py:96
  762.1 5.8 cholesky.163
  775.9 63.2 %all-gather.21.cloned.1.call-done = f32[32,576,64]{1,2,0:T(8,128)} async-done(((f32[1,576,64]{1,2,0:T(8,128)}), f32[32,576,64]{1,2,0:T(8,128)}) %all-gather.21.cloned.1.call-update) | async-done | bytes 4718608 | tf_op jit(solution)/shard_map/all_gather | solution.py:154
  839.1 7.8 copy.318
  846.9 6.4 reshape.73
  853.3 24.8 %fusion.101 = f32[576,64]{0,1:T(8,128)S(1)} fusion(f32[576,18432]{1,0:T(8,128)} %slice_dynamic-update-slice_fusion, f32[18432,64]{0,1:T(8,128)} %reshape.73), kind=kOutput, calls=%fused_computation.208 | convolution fusion | flops 4076863488 | bytes 47333376 | tf_op jit(solution)/shard_map/dot_general | solution.py:152
  880.1 19.4 %shard_map.63 = f32[128,128]{1,0:T(8,128)} custom-call(f32[576,64]{1,0:T(8,128)} %bitcast.211, f32[576,64]{1,0:T(8,128)} %copy.319.refs_1_), custom_call_target="tpu_custom_call" | custom-call | tf_op jit(solution)/shard_map/pallas_call | solution.py:96
  905.0 5.8 cholesky.174
  912.2 4.9 custom-call.16
  927.2 54.9 %all-gather.23.cloned.1.call-done = f32[32,576,64]{1,2,0:T(8,128)} async-done(((f32[1,576,64]{1,2,0:T(8,128)}), f32[32,576,64]{1,2,0:T(8,128)}) %all-gather.23.cloned.1.call-update) | async-done | bytes 4718608 | tf_op jit(solution)/shard_map/all_gather | solution.py:154
  982.1 7.9 copy.326
  989.9 6.3 reshape.75
  996.2 24.8 %fusion.102 = f32[576,64]{0,1:T(8,128)S(1)} fusion(f32[576,18432]{1,0:T(8,128)} %slice_dynamic-update-slice_fusion, f32[18432,64]{0,1:T(8,128)} %reshape.75), kind=kOutput, calls=%fused_computation.209 | convolution fusion | flops 4076863488 | bytes 47333376 | tf_op jit(solution)/shard_map/dot_general | solution.py:152
  1022.8 19.4 %shard_map.64 = f32[128,128]{1,0:T(8,128)} custom-call(f32[576,64]{1,0:T(8,128)} %bitcast.213, f32[576,64]{1,0:T(8,128)} %copy.327.refs_1_), custom_call_target="tpu_custom_call" | custom-call | tf_op jit(solution)/shard_map/pallas_call | solution.py:96
  1047.7 5.8 cholesky.185
  1057.2 4.9 custom-call.17
  (236 shorter events, 146.0 us)
Async XLA Ops:
  8.0 111.7 %all-reduce.2.cloned.1.call-start = ((), (), s32[]{:S(2)}) async-start(), calls=%async_computation | async-start | bytes 7077888 | tf_op jit(solution)/shard_map/psum | solution.py:125
  8.0 3.3 collective-permute-start
  11.4 6.2 collective-permute-start.1
  21.4 13.4 %copy-start.19 = (f32[576,64]{0,1:T(8,128)S(1)}, f32[576,64]{0,1:T(8,128)}, u32[]{:S(2)}) copy-start(f32[576,64]{0,1:T(8,128)} %param.6) | copy-start | bytes 442372
  21.5 0.9 copy-start.18
  34.3 234.1 %all-gather.13.cloned.1.call-start = ((), (), s32[]{:S(2)}) async-start(), calls=%async_computation.1 | async-start | bytes 5406720 | tf_op jit(solution)/shard_map/all_gather | solution.py:154
  69.5 6.3 copy-start.20
  76.1 1.7 copy-start.11
  76.3 1.5 copy-start
  77.1 334.5 %all-gather.15.cloned.1.call-start = ((), (), s32[]{:S(2)}) async-start(), calls=%async_computation.2 | async-start | bytes 5406720 | tf_op jit(solution)/shard_map/all_gather | solution.py:154
  282.8 48.5 %copy-start.12 = (f32[64,576]{1,0:T(8,128)S(1)}, f32[64,576]{1,0:T(8,128)}, u32[]{:S(2)}) copy-start(f32[64,576]{1,0:T(8,128)} %copy-done.11) | copy-start | bytes 442372
  347.3 72.1 %copy-start.2 = (f32[64,576]{0,1:T(8,128)}, f32[64,576]{0,1:T(8,128)S(1)}, u32[]{:S(2)}) copy-start(f32[64,576]{0,1:T(8,128)S(1)} %copy.292) | copy-start | bytes 442372
  348.2 206.0 %all-gather.17.cloned.1.call-start = ((), (), s32[]{:S(2)}) async-start(), calls=%async_computation.3 | async-start | bytes 5406720 | tf_op jit(solution)/shard_map/all_gather | solution.py:154
  489.8 72.3 %copy-start.4 = (f32[64,576]{0,1:T(8,128)}, f32[64,576]{0,1:T(8,128)S(1)}, u32[]{:S(2)}) copy-start(f32[64,576]{0,1:T(8,128)S(1)} %copy.300) | copy-start | bytes 442372
  490.6 206.1 %all-gather.19.cloned.1.call-start = ((), (), s32[]{:S(2)}) async-start(), calls=%async_computation.4 | async-start | bytes 5406720 | tf_op jit(solution)/shard_map/all_gather | solution.py:154
  632.2 72.3 %copy-start.6 = (f32[64,576]{0,1:T(8,128)}, f32[64,576]{0,1:T(8,128)S(1)}, u32[]{:S(2)}) copy-start(f32[64,576]{0,1:T(8,128)S(1)} %copy.308) | copy-start | bytes 442372
  633.1 206.0 %all-gather.21.cloned.1.call-start = ((), (), s32[]{:S(2)}) async-start(), calls=%async_computation.5 | async-start | bytes 5406720 | tf_op jit(solution)/shard_map/all_gather | solution.py:154
  774.6 72.3 %copy-start.8 = (f32[64,576]{0,1:T(8,128)}, f32[64,576]{0,1:T(8,128)S(1)}, u32[]{:S(2)}) copy-start(f32[64,576]{0,1:T(8,128)S(1)} %copy.316) | copy-start | bytes 442372
  775.4 206.6 %all-gather.23.cloned.1.call-start = ((), (), s32[]{:S(2)}) async-start(), calls=%async_computation.6 | async-start | bytes 5406720 | tf_op jit(solution)/shard_map/all_gather | solution.py:154
  853.3 65.2 %copy-start.21 = (f32[64,64]{1,0:T(8,128)S(1)}, f32[64,64]{1,0:T(8,128)}, u32[]{:S(2)}) copy-start(f32[64,64]{1,0:T(8,128)} %copy-done.20) | copy-start | bytes 49156
  853.3 65.8 %copy-start.1 = (f32[64,576]{0,1:T(8,128)S(1)}, f32[64,576]{0,1:T(8,128)}, u32[]{:S(2)}) copy-start(f32[64,576]{0,1:T(8,128)} %copy-done) | copy-start | bytes 442372
  878.1 41.8 %copy-start.13 = (f32[128,128]{1,0:T(8,128)S(1)}, f32[128,128]{1,0:T(8,128)}, u32[]{:S(2)}) copy-start(f32[128,128]{1,0:T(8,128)} %shard_map.59) | copy-start | bytes 196612
  878.1 42.5 %copy-start.3 = (f32[64,576]{0,1:T(8,128)S(1)}, f32[64,576]{0,1:T(8,128)}, u32[]{:S(2)}) copy-start(f32[64,576]{0,1:T(8,128)} %copy-done.2) | copy-start | bytes 442372
  878.1 44.0 %copy-start.14 = (f32[128,128]{1,0:T(8,128)S(1)}, f32[128,128]{1,0:T(8,128)}, u32[]{:S(2)}) copy-start(f32[128,128]{1,0:T(8,128)} %shard_map.60) | copy-start | bytes 196612
  878.1 44.0 %copy-start.5 = (f32[64,576]{0,1:T(8,128)S(1)}, f32[64,576]{0,1:T(8,128)}, u32[]{:S(2)}) copy-start(f32[64,576]{0,1:T(8,128)} %copy-done.4) | copy-start | bytes 442372
  878.1 45.4 %copy-start.15 = (f32[128,128]{1,0:T(8,128)S(1)}, f32[128,128]{1,0:T(8,128)}, u32[]{:S(2)}) copy-start(f32[128,128]{1,0:T(8,128)} %shard_map.61) | copy-start | bytes 196612
  878.1 45.4 %copy-start.7 = (f32[64,576]{0,1:T(8,128)S(1)}, f32[64,576]{0,1:T(8,128)}, u32[]{:S(2)}) copy-start(f32[64,576]{0,1:T(8,128)} %copy-done.6) | copy-start | bytes 442372
  878.2 46.8 %copy-start.16 = (f32[128,128]{1,0:T(8,128)S(1)}, f32[128,128]{1,0:T(8,128)}, u32[]{:S(2)}) copy-start(f32[128,128]{1,0:T(8,128)} %shard_map.62) | copy-start | bytes 196612
  878.2 46.8 %copy-start.9 = (f32[64,576]{0,1:T(8,128)S(1)}, f32[64,576]{0,1:T(8,128)}, u32[]{:S(2)}) copy-start(f32[64,576]{0,1:T(8,128)} %copy-done.8) | copy-start | bytes 442372
  899.4 26.9 %copy-start.17 = (f32[128,128]{1,0:T(8,128)S(1)}, f32[128,128]{1,0:T(8,128)}, u32[]{:S(2)}) copy-start(f32[128,128]{1,0:T(8,128)} %shard_map.63) | copy-start | bytes 196612
  917.6 72.3 %copy-start.10 = (f32[64,576]{0,1:T(8,128)}, f32[64,576]{0,1:T(8,128)S(1)}, u32[]{:S(2)}) copy-start(f32[64,576]{0,1:T(8,128)S(1)} %copy.324) | copy-start | bytes 442372
  1057.2 9.2 copy-start.22
Sparse Core Ops, SparseCore 0:
  34.4 85.3 all-reduce.1
Sparse Core Ops, SparseCore 1:
  77.2 69.4 all-gather.12
  348.3 63.2 all-gather.14
  490.7 63.5 all-gather.16
  633.2 63.5 all-gather.18
  775.5 63.5 all-gather.20
  918.5 63.5 all-gather.22
